TPU v7x, 32 devices: a whole 2x2x4 slice. The times are simulated.
32 devices in a mesh: group: 8 (over z, core), tensor: 4 (over y, x).
Axes of the slice: x: 2, y: 2, z: 4, core: 2. Of those that a mesh axis runs over, the one named last changes fastest.
Arguments:
- queries: bfloat16 [96, 4, 8192], P('group', None, 'tensor'), may hold values from -603 to 603
- new_entries: bfloat16 [96, 4, 2048], P('group'), may hold values from -6 to 6
- resident_cache: bfloat16 [32, 512, 2048], P('group', 'tensor'), may hold values from -6 to 6
- prefill_cache: bfloat16 [64, 512, 2048], P('group', 'tensor'), may hold values from -6 to 6
- resident_kept: int32 [32], replicated, may hold values from 256 to 512, as said below
- kept_tokens: int32 [64], replicated, may hold values from 1 to 512, as said below
- prefill_slot: int32 [64], replicated, may hold values from 0 to 63, as said below
- decode_slot: int32 [64], replicated, may hold values from 4 to 95, as said below
Outputs:
- attended: bfloat16 [96, 4, 8192], P('group', None, 'tensor')
Inputs may be any that keep to these rules, and one draw needn't show every extreme that they name: `kept_tokens`: some request keeps exactly 512 positions. `prefill_slot`: A permutation of the 64 prefill slots; slot s lies in prefill group s // 8. `decode_slot`: every slot g * 12 + l with l >= 4 is named by exactly one request; from one prefill group to one decode group go at most 1 request, and exactly 1 for some pairs. `resident_kept`: some resident request keeps exactly 512 positions.
All inputs are finite; a program needn't handle non-finite values.
Results may differ from a plain program's by a relative error of at most 0.0044.
Values may be sent and summed in bfloat16 or wider, within the bound.
A program may use at most 128 MiB of HBM per device.

v0:
```python
import math

import jax
import jax.numpy as jnp
from jax import lax
from jax.sharding import PartitionSpec as P

H = 64
KVH = 8
HD = 128
STEPS = 4
MIG_DEV = 8
RES_DEV = 4


NEG_FLOOR = -1e30


def routing(kept_tokens, prefill_slot, decode_slot, groups, per_pair):
    slot_count = MIG_DEV * groups
    per_group = RES_DEV + MIG_DEV
    dest_by_slot = jnp.zeros((slot_count,), jnp.int32).at[prefill_slot].set(decode_slot)
    kept_by_slot = jnp.zeros((slot_count,), jnp.int32).at[prefill_slot].set(kept_tokens)
    dest_group = (dest_by_slot // per_group).reshape(groups, MIG_DEV)
    earlier = jnp.arange(MIG_DEV)[None, :] < jnp.arange(MIG_DEV)[:, None]
    matching = dest_group[:, :, None] == dest_group[:, None, :]
    ranking = jnp.sum((matching & earlier[None]).astype(jnp.int32), axis=2)
    outgoing_row = (dest_group * per_pair + ranking).reshape(slot_count)
    source_by_dslot = jnp.zeros((groups * per_group,), jnp.int32).at[decode_slot].set(prefill_slot)
    return (kept_by_slot, ranking.reshape(slot_count), outgoing_row, source_by_dslot)


def partials(asking, stored, lengths, offset):
    row_count = stored.shape[0]
    stride = stored.shape[1]
    sharing = H // KVH
    asked_rows = asking.reshape(row_count, STEPS, KVH, sharing, HD)
    entries = stored.reshape(row_count, stride, 2, KVH, HD)
    scores = jnp.einsum(
        "rtkgd,rpkd->rtkgp", asked_rows, entries[:, :, 0], preferred_element_type=jnp.float32
    ) * (1.0 / math.sqrt(HD))
    usable = (offset + jnp.arange(stride))[None, :] < lengths[:, None]
    usable = usable[:, None, None, None, :]
    highest = jnp.max(jnp.where(usable, scores, NEG_FLOOR), axis=4)
    weights = jnp.where(usable, jnp.exp(scores - highest[..., None]), 0.0)
    totals = jnp.sum(weights, axis=4)
    blended = jnp.einsum(
        "rtkgp,rpkd->rtkgd",
        weights.astype(jnp.bfloat16),
        entries[:, :, 1],
        preferred_element_type=jnp.float32,
    )
    return (
        highest.reshape(row_count, STEPS, H),
        totals.reshape(row_count, STEPS, H),
        blended.reshape(row_count, STEPS, H, HD),
    )


def own_heads(parts):
    spread = (
        lax.all_to_all(parts[0][None], "tensor", split_axis=3, concat_axis=0, tiled=True),
        lax.all_to_all(parts[1][None], "tensor", split_axis=3, concat_axis=0, tiled=True),
        lax.all_to_all(parts[2][None], "tensor", split_axis=3, concat_axis=0, tiled=True),
    )
    highest = jnp.max(spread[0], axis=0)
    factors = jnp.exp(spread[0] - highest[None])
    totals = jnp.sum(spread[1] * factors, axis=0)
    blended = jnp.sum(spread[2] * factors[..., None], axis=0)
    result = (highest, totals, blended)
    return result


def body(
    queries,
    new_entries,
    resident_cache,
    prefill_cache,
    resident_kept,
    kept_tokens,
    prefill_slot,
    decode_slot,
):
    groups = lax.axis_size("group")
    shards = lax.axis_size("tensor")
    per_pair = max(1, MIG_DEV // groups)
    per_group = RES_DEV + MIG_DEV
    stride = prefill_cache.shape[1]
    features = prefill_cache.shape[2]
    offset = lax.axis_index("tensor") * stride
    group_here = lax.axis_index("group")
    kept_by_slot, ranking, outgoing_row, source_by_dslot = routing(
        kept_tokens, prefill_slot, decode_slot, groups, per_pair
    )
    local_rows = lax.dynamic_slice_in_dim(outgoing_row, group_here * MIG_DEV, MIG_DEV)
    arriving = lax.dynamic_slice_in_dim(source_by_dslot, group_here * per_group + RES_DEV, MIG_DEV)
    arriving_rows = arriving // MIG_DEV * per_pair + ranking[arriving]
    arriving_kept = kept_by_slot[arriving]
    resident_len = lax.dynamic_slice_in_dim(resident_kept, group_here * RES_DEV, RES_DEV)
    asking = lax.all_gather(queries, "tensor", axis=2, tiled=True)
    resident_parts = partials(asking[:RES_DEV], resident_cache, resident_len, offset)
    outgoing = (
        jnp.zeros((groups * per_pair, stride, features), jnp.bfloat16)
        .at[local_rows]
        .set(prefill_cache)
    )
    arrived = lax.all_to_all(
        outgoing.reshape(groups, per_pair, stride, features),
        "group",
        split_axis=0,
        concat_axis=0,
        tiled=True,
    )
    moved_cache = arrived.reshape(groups * per_pair, stride, features)[arriving_rows]
    moved_parts = partials(asking[RES_DEV:], moved_cache, arriving_kept, offset)
    heads_parts = own_heads(
        tuple(
            (
                jnp.concatenate([former, latter], 0)
                for former, latter in zip(resident_parts, moved_parts)
            )
        )
    )
    highest, totals, blended = heads_parts
    stride_heads = H // shards
    sharing = H // KVH
    heads_here = lax.axis_index("tensor") * stride_heads + jnp.arange(stride_heads)
    pairs_here = heads_here // sharing
    asked_here = queries.reshape(per_group, STEPS, stride_heads, HD)
    newest = new_entries.reshape(per_group, STEPS, 2, KVH, HD)
    new_keys = jnp.take(newest[:, :, 0], pairs_here, axis=2)
    new_values = jnp.take(newest[:, :, 1], pairs_here, axis=2)
    scores = jnp.einsum(
        "rthd,ruhd->rthu", asked_here, new_keys, preferred_element_type=jnp.float32
    ) * (1.0 / math.sqrt(HD))
    causal = (jnp.arange(STEPS)[None, :] <= jnp.arange(STEPS)[:, None])[None, :, None, :]
    new_high = jnp.max(jnp.where(causal, scores, NEG_FLOOR), axis=3)
    overall = jnp.maximum(highest, new_high)
    weights = jnp.where(causal, jnp.exp(scores - overall[..., None]), 0.0)
    carried = jnp.exp(highest - overall)
    totals = totals * carried + jnp.sum(weights, axis=3)
    blended = blended * carried[..., None] + jnp.einsum(
        "rthu,ruhd->rthd",
        weights.astype(jnp.bfloat16),
        new_values,
        preferred_element_type=jnp.float32,
    )
    return (
        (blended / totals[..., None])
        .astype(jnp.bfloat16)
        .reshape(per_group, STEPS, stride_heads * HD)
    )


def solution(mesh):
    in_specs = (
        P("group", None, "tensor"),
        P("group", None, None),
        P("group", "tensor", None),
        P("group", "tensor", None),
        P(),
        P(),
        P(),
        P(),
    )
    out_specs = P("group", None, "tensor")
    return jax.shard_map(body, mesh=mesh, in_specs=in_specs, out_specs=out_specs, check_vma=False)
```

profile of v0, /device:TPU:0, one launch (start us, length us, event | category | flops | bytes accessed | tf_op | source)
XLA Modules:
  0.0 171.6 jit_solution(17943824159016602118)
XLA Ops:
  0.0 0.7 compare_select_fusion.4
  0.7 0.9 scatter_custom_fusion
  1.7 0.3 convert_reduce_fusion
  2.1 2.5 %broadcast_in_dim.119 = bf16[8,128,2048]{2,1,0:T(8,128)(2,1)} broadcast(bf16[]{:T(256)} %constant.76.clone.1), dimensions={} | broadcast | bytes 4194306 | tf_op jit(solution)/shard_map/broadcast_in_dim | solution.py:103
  4.6 10.9 %scatter_fusion = bf16[8,128,2048]{2,1,0:T(8,128)(2,1)} fusion(bf16[8,128,2048]{2,1,0:T(8,128)(2,1)} %broadcast_in_dim.119, s32[8]{0:T(128)S(1)} %compare_select_fusion.3, bf16[8,128,2048]{2,1,0:T(8,128)(2,1)} %param.13), kind=kCustom, calls=%fused_computation.6 | custom fusion | bytes 12582944 | tf_op jit(solution)/shard_map/scatter | solution.py:105
  15.6 6.5 %all-to-all-start = ((bf16[8,1,128,2048]{3,2,1,0:T(8,128)(2,1)}), bf16[8,1,128,2048]{3,2,1,0:T(8,128)(2,1)}, u32[]{:S(2)}, u32[]{:S(2)}) async-start(bf16[8,1,128,2048]{3,2,1,0:T(8,128)(2,1)} %bitcast.150), calls=%async_computation | async-start | bytes 8388608 | tf_op jit(solution)/shard_map/all_to_all | solution.py:107
  22.1 13.1 %all_gather.3 = bf16[12,4,8192]{2,1,0:T(4,128)(2,1)S(1)} all-gather(bf16[12,4,2048]{2,1,0:T(4,128)(2,1)S(1)} %copy-done.3), channel_id=1, replica_groups=mesh['group'=8,'tensor'=4] {'tensor'}, dimensions={2}, use_global_device_ids=true | all-gather | bytes 983040 | tf_op jit(solution)/shard_map/all_gather | solution.py:100
  35.2 0.2 slice.47
  35.4 0.1 slice.43
  35.5 1.0 scatter_custom_fusion.2
  36.6 0.6 gather_fusion
  37.3 0.9 scatter_custom_fusion.3
  38.2 0.6 gather_fusion.2
  38.8 1.4 reshape.264
  40.2 2.5 %copy.189 = bf16[4,128,2048]{1,2,0:T(8,128)(2,1)} copy(bf16[4,128,2048]{2,1,0:T(8,128)(2,1)S(1)} %copy-done.1) | data formatting | bytes 4194304 | tf_op args[2]
  42.7 0.3 reshape.161
  43.2 0.4 copy-done.7
  43.6 1.9 %select_reduce_fusion.1 = (f32[4,4,8,8]{3,1,2,0:T(4,128)S(1)}, f32[4,4,8,8,128]{4,3,1,2,0:T(8,128)S(1)}) fusion(pred[4,128]{1,0:T(4,128)(4,1)S(1)} %broadcast_compare_fusion.1, bf16[4,4,8,8,128]{4,3,2,1,0:T(8,128)(2,1)S(1)} %reshape.161, bf16[4,128,2,8,128]{1,4,3,2,0:T(8,128)(2,1)} %bitcast.155), kind=kOutput, calls=%fused_computation.39 | convolution fusion | flops 33946624 | bytes 1839616 | tf_op jit(solution)/shard_map/rtkgd,rpkd->rtkgp/dot_general | solution.py:39
  45.5 0.4 fusion.18
  46.1 0.2 copy-done.5
  46.3 0.1 reshape.170
  46.6 0.8 gather_fusion.3
  47.4 0.8 gather_fusion.4
  48.2 1.7 %convolution_bitcast_fusion = f32[4,4,8,8,128]{4,3,1,2,0:T(8,128)S(1)} fusion(bf16[4,128,2,8,128]{1,4,3,2,0:T(8,128)(2,1)S(1)} %bitcast.156, f32[4,4,8,8,128]{4,3,1,2,0:T(8,128)} %copy-done.5, f32[4,4,8,8]{3,1,2,0:T(4,128)S(1)} %get-tuple-element.18, pred[4,128]{1,0:T(4,128)(4,1)S(1)} %broadcast_compare_fusion.1), kind=kOutput, calls=%fused_computation.21 | convolution fusion | flops 33947648 | bytes 2163200 | tf_op jit(solution)/shard_map/rtkgp,rpkd->rtkgd/dot_general | solution.py:47
  50.0 0.1 compare_select_fusion.1
  50.2 0.2 select_bitcast_fusion
  50.4 65.7 %all-to-all-done = bf16[8,1,128,2048]{3,2,1,0:T(8,128)(2,1)} async-done(((bf16[8,1,128,2048]{3,2,1,0:T(8,128)(2,1)}), bf16[8,1,128,2048]{3,2,1,0:T(8,128)(2,1)}, u32[]{:S(2)}, u32[]{:S(2)}) %all-to-all-start) | async-done | bytes 4194336 | tf_op jit(solution)/shard_map/all_to_all | solution.py:107
  116.2 5.0 %gather_fusion.1 = bf16[8,128,2048]{2,1,0:T(8,128)(2,1)} fusion(bf16[8,128,2048]{2,1,0:T(8,128)(2,1)} %bitcast.12, s32[1024]{0:T(1024)S(1)} %pad_clamp_fusion.1), kind=kCustom, calls=%fused_computation.3 | custom fusion | bytes 8388640 | tf_op jit(solution)/shard_map/gather | solution.py:114
  121.1 6.5 %copy.195 = bf16[8,128,2048]{1,2,0:T(8,128)(2,1)} copy(bf16[8,128,2048]{2,1,0:T(8,128)(2,1)} %gather_fusion.1) | data formatting | bytes 8388608 | tf_op jit(solution)/shard_map/gather | solution.py:114
  127.6 2.5 %select_reduce_fusion = (f32[8,4,8,8]{3,1,2,0:T(4,128)S(1)}, f32[8,4,8,8,128]{4,3,1,2,0:T(8,128)S(1)}) fusion(pred[8,128]{1,0:T(8,128)(4,1)S(1)} %broadcast_compare_fusion, bf16[8,4,8,8,128]{4,3,2,1,0:T(8,128)(2,1)S(1)} %copy-done.4, bf16[8,128,2,8,128]{1,4,3,2,0:T(8,128)(2,1)} %bitcast.153), kind=kOutput, calls=%fused_computation.31 | convolution fusion | flops 67893248 | bytes 3679232 | tf_op jit(solution)/shard_map/rtkgd,rpkd->rtkgp/dot_general | solution.py:39
  130.2 0.8 fusion.11
  130.9 1.2 fusion.3
  132.2 0.1 reshape.173
  132.3 0.1 copy.222
  132.5 0.8 reshape.275
  133.2 3.7 %all-to-all-start.3 = ((f32[4,1,768]{2,1,0:T(1,128)}), f32[4,1,768]{2,1,0:T(1,128)S(1)}, u32[]{:S(2)}, u32[]{:S(2)}) async-start(f32[4,1,768]{2,1,0:T(1,128)} %reshape.275), calls=%async_computation.3 | async-start | bytes 24576 | tf_op jit(solution)/shard_map/all_to_all | solution.py:63
  137.0 0.1 reshape.169
  137.1 0.1 copy.206
  137.2 0.8 reshape.273
  138.0 0.1 copy.267
  138.1 3.5 %all-to-all-done.3 = f32[4,1,768]{2,1,0:T(1,128)S(1)} async-done(((f32[4,1,768]{2,1,0:T(1,128)}), f32[4,1,768]{2,1,0:T(1,128)S(1)}, u32[]{:S(2)}, u32[]{:S(2)}) %all-to-all-start.3) | async-done | bytes 12320 | tf_op jit(solution)/shard_map/all_to_all | solution.py:63
  141.7 3.3 %all-to-all-start.2 = ((f32[4,1,768]{2,1,0:T(1,128)}), f32[4,1,768]{2,1,0:T(1,128)S(1)}, u32[]{:S(2)}, u32[]{:S(2)}) async-start(f32[4,1,768]{2,1,0:T(1,128)} %reshape.273), calls=%async_computation.2 | async-start | bytes 24576 | tf_op jit(solution)/shard_map/all_to_all | solution.py:62
  144.9 0.2 maximum_bitcast_fusion
  145.1 2.2 %copy.201 = f32[1,12,4,64,128]{4,2,1,0,3:T(4,128)} copy(f32[1,12,4,64,128]{4,3,2,1,0:T(8,128)S(1)} %maximum_bitcast_fusion) | data formatting | bytes 3145728 | tf_op jit(solution)/shard_map/broadcast_in_dim | solution.py:64
  147.3 2.3 %all-to-all-done.2 = f32[4,1,768]{2,1,0:T(1,128)S(1)} async-done(((f32[4,1,768]{2,1,0:T(1,128)}), f32[4,1,768]{2,1,0:T(1,128)S(1)}, u32[]{:S(2)}, u32[]{:S(2)}) %all-to-all-start.2) | async-done | bytes 12320 | tf_op jit(solution)/shard_map/all_to_all | solution.py:62
  149.6 3.7 %all-to-all-start.1 = ((f32[1,12,4,64,128]{4,2,1,0,3:T(4,128)}), f32[1,12,4,64,128]{4,2,1,0,3:T(4,128)S(1)}, u32[]{:S(2)}, u32[]{:S(2)}) async-start(f32[1,12,4,64,128]{4,2,1,0,3:T(4,128)} %copy.201), calls=%async_computation.1 | async-start | bytes 3145728 | tf_op jit(solution)/shard_map/all_to_all | solution.py:64
  153.3 0.3 fusion.25
  153.7 0.4 copy.211
  154.1 0.2 fusion.31
  154.2 0.5 broadcast.174
  154.7 0.7 reduce.2
  155.4 0.2 reshape.276
  155.6 0.2 copy.236
  155.8 0.7 reduce.1
  156.5 0.2 reshape.274
  156.7 0.2 copy.234
  157.0 0.2 fusion.34
  157.2 0.1 fusion.29
  157.3 0.1 copy.214
  157.4 0.1 copy.226
  157.6 0.4 copy.218
  158.0 11.8 %all-to-all-done.1 = f32[1,12,4,64,128]{4,2,1,0,3:T(4,128)S(1)} async-done(((f32[1,12,4,64,128]{4,2,1,0,3:T(4,128)}), f32[1,12,4,64,128]{4,2,1,0,3:T(4,128)S(1)}, u32[]{:S(2)}, u32[]{:S(2)}) %all-to-all-start.1) | async-done | bytes 1572896 | tf_op jit(solution)/shard_map/all_to_all | solution.py:64
  169.8 0.6 fusion.2
  170.4 1.2 fusion.10
  (52 shorter events, 1.2 us)
Async XLA Ops:
  15.6 6.5 %copy-start.3 = (bf16[12,4,2048]{2,1,0:T(4,128)(2,1)S(1)}, bf16[12,4,2048]{2,1,0:T(4,128)(2,1)}, u32[]{:S(2)}) copy-start(bf16[12,4,2048]{2,1,0:T(4,128)(2,1)} %param.10) | copy-start | bytes 589828
  15.6 100.6 %all-to-all-start = ((bf16[8,1,128,2048]{3,2,1,0:T(8,128)(2,1)}), bf16[8,1,128,2048]{3,2,1,0:T(8,128)(2,1)}, u32[]{:S(2)}, u32[]{:S(2)}) async-start(bf16[8,1,128,2048]{3,2,1,0:T(8,128)(2,1)} %bitcast.150), calls=%async_computation | async-start | bytes 8388608 | tf_op jit(solution)/shard_map/all_to_all | solution.py:107
  22.1 13.4 %copy-start.9 = (s32[64]{0:T(128)S(1)}, s32[64]{0:T(128)}, u32[]{:S(2)}) copy-start(s32[64]{0:T(128)} %param.17) | copy-start | bytes 772
  35.2 5.0 %copy-start.1 = (bf16[4,128,2048]{2,1,0:T(8,128)(2,1)S(1)}, bf16[4,128,2048]{2,1,0:T(8,128)(2,1)}, u32[]{:S(2)}) copy-start(bf16[4,128,2048]{2,1,0:T(8,128)(2,1)} %param.12) | copy-start | bytes 6291460
  40.2 2.8 %copy-start.10 = (s32[32]{0:T(128)S(1)}, s32[32]{0:T(128)}, u32[]{:S(2)}) copy-start(s32[32]{0:T(128)} %param.14) | copy-start | bytes 388
  42.7 3.6 %copy-start.6 = (bf16[12,4,2048]{2,1,0:T(4,128)(2,1)S(1)}, bf16[12,4,2048]{2,1,0:T(4,128)(2,1)}, u32[]{:S(2)}) copy-start(bf16[12,4,2048]{2,1,0:T(4,128)(2,1)} %param.11) | copy-start | bytes 589828
  43.1 0.5 copy-start.7
  43.6 4.5 %copy-start.2 = (bf16[4,128,2048]{1,2,0:T(8,128)(2,1)S(1)}, bf16[4,128,2048]{1,2,0:T(8,128)(2,1)}, u32[]{:S(2)}) copy-start(bf16[4,128,2048]{1,2,0:T(8,128)(2,1)} %copy.189) | copy-start | bytes 6291460
  45.5 0.8 copy-start.5
  46.6 3.5 %copy-start.8 = (s32[128]{0:T(128)S(1)}, s32[128]{0:T(128)}, u32[]{:S(2)}) copy-start(s32[128]{0:T(128)} %copy-done.7) | copy-start | bytes 1540
  121.1 6.5 %copy-start.4 = (bf16[8,4,8,8,128]{4,3,2,1,0:T(8,128)(2,1)S(1)}, bf16[8,4,8,8,128]{4,3,2,1,0:T(8,128)(2,1)}, u32[]{:S(2)}) copy-start(bf16[8,4,8,8,128]{4,3,2,1,0:T(8,128)(2,1)} %reshape.264) | copy-start | bytes 1572868
  127.6 3.3 %copy-start = (bf16[8,128,2048]{1,2,0:T(8,128)(2,1)S(1)}, bf16[8,128,2048]{1,2,0:T(8,128)(2,1)}, u32[]{:S(2)}) copy-start(bf16[8,128,2048]{1,2,0:T(8,128)(2,1)} %copy.195) | copy-start | bytes 12582916
  133.2 8.4 %all-to-all-start.3 = ((f32[4,1,768]{2,1,0:T(1,128)}), f32[4,1,768]{2,1,0:T(1,128)S(1)}, u32[]{:S(2)}, u32[]{:S(2)}) async-start(f32[4,1,768]{2,1,0:T(1,128)} %reshape.275), calls=%async_computation.3 | async-start | bytes 24576 | tf_op jit(solution)/shard_map/all_to_all | solution.py:63
  141.7 7.9 %all-to-all-start.2 = ((f32[4,1,768]{2,1,0:T(1,128)}), f32[4,1,768]{2,1,0:T(1,128)S(1)}, u32[]{:S(2)}, u32[]{:S(2)}) async-start(f32[4,1,768]{2,1,0:T(1,128)} %reshape.273), calls=%async_computation.2 | async-start | bytes 24576 | tf_op jit(solution)/shard_map/all_to_all | solution.py:62
  149.6 20.2 %all-to-all-start.1 = ((f32[1,12,4,64,128]{4,2,1,0,3:T(4,128)}), f32[1,12,4,64,128]{4,2,1,0,3:T(4,128)S(1)}, u32[]{:S(2)}, u32[]{:S(2)}) async-start(f32[1,12,4,64,128]{4,2,1,0,3:T(4,128)} %copy.201), calls=%async_computation.1 | async-start | bytes 3145728 | tf_op jit(solution)/shard_map/all_to_all | solution.py:64
where the time goes:
time: 172 us
  waiting for transfers between devices  83.4 us (48%)
  local copies, waits for them, and re-layouts  43 us (25%)
  starting transfers between devices  17.2 us (10%)
  blocking collectives  13.1 us (8%)
  matrix products  8.87 us (5%)
  other arithmetic  5.57 us (3%)
    all_to_all x1, waiting for transfers between devices, body(): lax.all_to_all(outgoing.reshape(groups, per_pair, stride, features), 'gro...  65.7 us
    all_gather x1, blocking collectives, body(): asking = lax.all_gather(queries, 'tensor', axis=2, tiled=True)  13.1 us
    all_to_all x1, waiting for transfers between devices, own_heads(): lax.all_to_all(parts[2][None], 'tensor', split_axis=3, concat_axis=0, til...  11.8 us
    gather x2, local copies, waits for them, and re-layouts, body(): arrived.reshape(groups * per_pair, stride, features)[arriving_rows]  11.5 us
    scatter x1, local copies, waits for them, and re-layouts, body(): outgoing = jnp.zeros((groups * per_pair, stride, features), jnp.bfloat16)...  10.9 us
    all_to_all x1, starting transfers between devices, body(): lax.all_to_all(outgoing.reshape(groups, per_pair, stride, features), 'gro...  6.49 us
    unnamed x27, local copies, waits for them, and re-layouts  5.1 us
    dot_general x2, matrix products, partials(): jnp.einsum('rtkgd,rpkd->rtkgp', asked_rows, entries[:, :, 0], preferred_e...  4.38 us
  transfers between devices with their start and end apart: 4, of which 4 were waited for; matrix products, arithmetic and copies ran while one was open for 13% of the time, Pallas kernels for 0%

commit v1 on v0

v1 whole, which is shorter than its diff:
```python
import functools
import math

import jax
import jax.numpy as jnp
from jax import lax
from jax.experimental import pallas as pl
from jax.experimental.pallas import tpu as pltpu
from jax.sharding import PartitionSpec as P

H = 64
KVH = 8
HD = 128
STEPS = 4
MIG_DEV = 8
RES_DEV = 4
PER_GROUP = RES_DEV + MIG_DEV
BATCH = 4

NEG_FLOOR = -1e30
SCALE = 1.0 / math.sqrt(HD)
MESH = pl.DeviceIdType.MESH
F32 = jnp.float32
BF16 = jnp.bfloat16
NT = (((1,), (1,)), ((), ()))
TN = (((0,), (0,)), ((), ()))


def kernel(
    G,
    T,
    tbl,
    kept,
    q_in,
    new_in,
    res_hbm,
    pre_hbm,
    out,
    res,
    pre,
    qall,
    zq,
    stage,
    obuf,
    rbuf,
    sbuf,
    rstat,
    statbuf,
    facbuf,
    zo,
    zro,
    zs,
    zrs,
    newk,
    fin,
    cache_sem,
    zq_s,
    zq_r,
    rq_s,
    rq_r,
    f_s,
    f_r,
    o_s,
    o_r,
    st_s,
    st_r,
    zo_s,
    zo_r,
    zs_s,
    zs_r,
):
    KVL = max(1, KVH // T)
    HB = H // T
    HU = HB // KVL
    R = STEPS * HU
    LW = BATCH * R
    SW = 2 * KVL
    NB = 1 + G // BATCH
    pos = res.shape[1]
    half = KVH * HD
    g = lax.axis_index("group")
    t = lax.axis_index("tensor")
    offset = t * pos

    def peer_t(k):
        return lax.rem(t + k, T)

    def peer_g(k):
        return lax.rem(g + k, G)

    def from_g(k):
        return lax.rem(g - k + G, G)

    def over_t(src, dst, ssem, rsem, dev):
        return pltpu.make_async_remote_copy(
            src_ref=src, dst_ref=dst, send_sem=ssem, recv_sem=rsem,
            device_id=(g, dev), device_id_type=MESH,
        )

    def over_g(src, dst, ssem, rsem, dev):
        return pltpu.make_async_remote_copy(
            src_ref=src, dst_ref=dst, send_sem=ssem, recv_sem=rsem,
            device_id=(dev, t), device_id_type=MESH,
        )

    def c_zq(k):
        return over_g(zq.at[k], qall.at[t, RES_DEV + k], zq_s.at[k], zq_r.at[k], peer_g(k))

    def c_rq(k):
        p = peer_t(k)
        own = qall.at[t, pl.ds(0, RES_DEV)]
        return over_t(own, own, rq_s.at[k], rq_r.at[k], p)

    def c_fwd(k, n):
        own = qall.at[t, RES_DEV + k]
        return over_t(own, own, f_s.at[k, n], f_r.at[k, n], peer_t(n))

    def c_o(b, n):
        p = peer_t(n)
        return over_t(obuf.at[b, p], rbuf.at[b, n], o_s.at[b, n], o_r.at[b, n], p)

    def c_st(b, n):
        p = peer_t(n)
        return over_t(sbuf.at[b, p], rstat.at[b, n], st_s.at[b, n], st_r.at[b, n], p)

    def c_zo(k):
        return over_g(zo.at[k], zro.at[k], zo_s.at[k], zo_r.at[k], from_g(k))

    def c_zs(k):
        return over_g(zs.at[k // BATCH], zrs.at[k], zs_s.at[k], zs_r.at[k], from_g(k))

    load_res = pltpu.make_async_copy(res_hbm, res, cache_sem.at[0])
    load_pre = pltpu.make_async_copy(pre_hbm, pre, cache_sem.at[1])
    load_res.start()
    load_pre.start()

    barrier = pltpu.get_barrier_semaphore()
    for k in range(1, G):
        pl.semaphore_signal(barrier, inc=1, device_id=(peer_g(k), t), device_id_type=MESH)
    for k in range(1, T):
        pl.semaphore_signal(barrier, inc=1, device_id=(g, peer_t(k)), device_id_type=MESH)

    def arranged(row, slot):
        for h in range(HB):
            piece = q_in[row, :, h * HD : (h + 1) * HD]
            stage[slot, h * STEPS : (h + 1) * STEPS, :] = piece.astype(F32)
        return stage[slot].astype(BF16)

    for k in range(G):
        block = arranged(tbl[0, peer_g(k)], k)
        zq[k] = block
        if k == 0:
            qall[t, RES_DEV] = block
    for j in range(RES_DEV):
        qall[t, j] = arranged(j, G + j)

    pl.semaphore_wait(barrier, G - 1 + T - 1)
    for k in range(1, G):
        c_zq(k).start()
    for n in range(1, T):
        c_rq(n).start()
    for n in range(1, T):
        c_fwd(0, n).start()

    kv_col = pl.multiple_of((t * KVL * KVH) // (T * KVL) * HD, HD)
    for b in range(NB):
        for j in range(BATCH):
            row = j if b == 0 else tbl[0, peer_g((b - 1) * BATCH + j)]
            lo = j * STEPS
            newk[b, 0, lo : lo + STEPS, :] = new_in[row, :, pl.ds(kv_col, KVL * HD)].astype(F32)
            newk[b, 1, lo : lo + STEPS, :] = new_in[
                row, :, pl.ds(pl.multiple_of(half + kv_col, HD), KVL * HD)
            ].astype(F32)

    for k in range(1, G):
        c_zq(k).wait_recv()
        for n in range(1, T):
            c_fwd(k, n).start()

    def attend_slot(cache, row, length, slot, b, j):
        lane = lax.broadcasted_iota(jnp.int32, (R, 128), 1)
        usable = offset + lax.broadcasted_iota(jnp.int32, (R, pos), 1) < length
        stat = jnp.zeros((R, 128), F32)
        rows = pl.ds(pl.multiple_of(j * R, R), R)
        for tt in range(T):
            for i in range(KVL):
                kv = (tt * KVL + i) * KVH // (T * KVL)
                asked = qall[tt, slot, i * R : (i + 1) * R, :]
                keys = cache[row, :, kv * HD : (kv + 1) * HD]
                values = cache[row, :, half + kv * HD : half + (kv + 1) * HD]
                scores = lax.dot_general(asked, keys, NT, preferred_element_type=F32) * SCALE
                scores = jnp.where(usable, scores, NEG_FLOOR)
                highest = jnp.max(scores, axis=1, keepdims=True)
                weights = jnp.where(usable, jnp.exp(scores - highest), 0.0)
                total = jnp.sum(weights, axis=1, keepdims=True)
                blended = jnp.dot(weights.astype(BF16), values, preferred_element_type=F32)
                obuf[b, tt, i, rows, :] = blended.astype(BF16)
                stat = jnp.where(lane == tt * SW + i, highest, stat)
                stat = jnp.where(lane == tt * SW + KVL + i, total, stat)
        statbuf[rows, :] = stat

    def send_batch(b):
        turned = statbuf[...].T
        for tt in range(T):
            sbuf[b, tt] = turned[tt * SW : tt * SW + 8, :]
        for n in range(1, T):
            c_st(b, n).start()
            c_o(b, n).start()
        rbuf[b, 0] = obuf[b, t]
        rstat[b, 0] = sbuf[b, t]

    load_res.wait()
    for n in range(1, T):
        c_rq(n).wait_recv()

    @pl.loop(0, RES_DEV)
    def _(j):
        attend_slot(res, j, kept[g * RES_DEV + j], j, 0, j)

    send_batch(0)
    load_pre.wait()

    @pl.loop(1, NB)
    def _(b):
        @pl.loop(0, BATCH)
        def _(j):
            k = (b - 1) * BATCH + j
            for n in range(1, T):
                c_fwd(k, n).wait_recv()
            source = from_g(k)
            attend_slot(pre, tbl[1, source], tbl[2, source], RES_DEV + k, b, j)

        send_batch(b)

    def merged(b):
        for n in range(1, T):
            c_st(b, n).wait_recv()
            c_o(b, n).wait_recv()
        tops = [rstat[b, n][:KVL] for n in range(T)]
        highest = functools.reduce(jnp.maximum, tops)
        total = jnp.zeros((KVL, LW), F32)
        for n in range(T):
            factor = jnp.exp(tops[n] - highest)
            total = total + factor * rstat[b, n][KVL:SW]
            facbuf[n * KVL : (n + 1) * KVL, :] = factor
        columns = facbuf[...].T
        blended = []
        for i in range(KVL):
            sum_i = jnp.zeros((LW, HD), F32)
            for n in range(T):
                c = n * KVL + i
                sum_i = sum_i + rbuf[b, n, i].astype(F32) * columns[:, c : c + 1]
            blended.append(sum_i)
        return highest, total, blended

    def finish(b, highest, total, blended, asked):
        r16 = lax.broadcasted_iota(jnp.int32, (BATCH * STEPS, LW), 0)
        lanes = lax.broadcasted_iota(jnp.int32, (BATCH * STEPS, LW), 1)
        causal = (r16 // STEPS == lanes // R) & (r16 % STEPS <= lanes % STEPS)
        adds = []
        for i in range(KVL):
            keys = newk[b, 0, :, i * HD : (i + 1) * HD].astype(BF16)
            values = newk[b, 1, :, i * HD : (i + 1) * HD].astype(BF16)
            scores = lax.dot_general(keys, asked[i], NT, preferred_element_type=F32) * SCALE
            scores = jnp.where(causal, scores, NEG_FLOOR)
            top = jnp.maximum(highest[i : i + 1], jnp.max(scores, axis=0, keepdims=True))
            weights = jnp.where(causal, jnp.exp(scores - top), 0.0)
            carried = jnp.exp(highest[i : i + 1] - top)
            inverse = 1.0 / (total[i : i + 1] * carried + jnp.sum(weights, axis=0, keepdims=True))
            facbuf[i : i + 1, :] = carried
            facbuf[KVL + i : KVL + i + 1, :] = inverse
            adds.append(
                lax.dot_general(weights.astype(BF16), values, TN, preferred_element_type=F32)
            )
        columns = facbuf[...].T
        for i in range(KVL):
            done = blended[i] * columns[:, i : i + 1] + adds[i]
            done = done * columns[:, KVL + i : KVL + i + 1]
            for j in range(BATCH):
                fin[b * BATCH + j, i * R : (i + 1) * R, :] = done[j * R : (j + 1) * R]

    def put(slot, row):
        for h in range(HB):
            piece = fin[slot, h * STEPS : (h + 1) * STEPS, :]
            out[row, :, h * HD : (h + 1) * HD] = piece.astype(BF16)

    for b in range(1, NB):
        highest, total, blended = merged(b)
        packed = jnp.concatenate([highest, total], axis=0)
        zs[b - 1, 0:SW, :] = packed
        for j in range(BATCH):
            k = (b - 1) * BATCH + j
            for i in range(KVL):
                zo[k, i] = blended[i][j * R : (j + 1) * R].astype(BF16)
            if k:
                c_zs(k).start()
                c_zo(k).start()
            else:
                zrs[0] = zs[0]
                zro[0] = zo[0]

    def queries_of(b):
        return [
            jnp.concatenate(
                [
                    (qall[t, j] if b == 0 else zq[(b - 1) * BATCH + j])[i * R : (i + 1) * R]
                    for j in range(BATCH)
                ],
                axis=0,
            )
            for i in range(KVL)
        ]

    finish(0, *merged(0), queries_of(0))
    for j in range(RES_DEV):
        put(j, j)

    for b in range(1, NB):
        lanes = lax.broadcasted_iota(jnp.int32, (8, LW), 1)
        stats = jnp.zeros((8, LW), F32)
        for j in range(BATCH):
            k = (b - 1) * BATCH + j
            if k:
                c_zs(k).wait_recv()
                c_zo(k).wait_recv()
            stats = jnp.where(lanes // R == j, zrs[k], stats)
        blended = [
            jnp.concatenate(
                [zro[(b - 1) * BATCH + j, i].astype(F32) for j in range(BATCH)], axis=0
            )
            for i in range(KVL)
        ]
        finish(b, stats[:KVL], stats[KVL:SW], blended, queries_of(b))
    for l in range(MIG_DEV):
        put(RES_DEV + tbl[3, l], RES_DEV + l)

    for k in range(1, G):
        c_zq(k).wait_send()
        c_zs(k).wait_send()
        c_zo(k).wait_send()
    for n in range(1, T):
        c_rq(n).wait_send()

        @pl.loop(0, G)
        def _(k):
            c_fwd(k, n).wait_send()

        @pl.loop(0, NB)
        def _(b):
            c_st(b, n).wait_send()
            c_o(b, n).wait_send()


def routes(kept_tokens, prefill_slot, decode_slot, G):
    g = lax.axis_index("group")
    dest_group, dest_row = decode_slot // PER_GROUP, decode_slot % PER_GROUP
    home_group, home_row = prefill_slot // MIG_DEV, prefill_slot % MIG_DEV
    arriving, leaving = dest_group == g, home_group == g
    width = max(G, MIG_DEV)
    every = jnp.arange(width, dtype=jnp.int32)[:, None]

    def pick(key, wanted, value):
        hit = (key[None] == every) & wanted[None]
        return jnp.sum(jnp.where(hit, value[None], 0), axis=1)

    return jnp.stack(
        [
            pick(home_group, arriving, dest_row),
            pick(dest_group, leaving, home_row),
            pick(dest_group, leaving, kept_tokens),
            pick(dest_row - RES_DEV, arriving, (home_group - g + G) % G),
        ]
    )


def body(
    queries,
    new_entries,
    resident_cache,
    prefill_cache,
    resident_kept,
    kept_tokens,
    prefill_slot,
    decode_slot,
):
    G = lax.axis_size("group")
    T = lax.axis_size("tensor")
    KVL = max(1, KVH // T)
    HB = H // T
    RB = STEPS * HB
    R = RB // KVL
    LW = BATCH * R
    NB = 1 + G // BATCH
    tbl = routes(kept_tokens, prefill_slot, decode_slot, G)
    dma = pltpu.SemaphoreType.DMA
    vmem = pl.BlockSpec(memory_space=pltpu.VMEM)
    smem = pl.BlockSpec(memory_space=pltpu.SMEM)
    hbm = pl.BlockSpec(memory_space=pl.ANY)
    return pl.pallas_call(
        functools.partial(kernel, G, T),
        out_shape=jax.ShapeDtypeStruct(queries.shape, BF16),
        in_specs=[smem, smem, vmem, vmem, hbm, hbm],
        out_specs=vmem,
        scratch_shapes=[
            pltpu.VMEM(resident_cache.shape, BF16),
            pltpu.VMEM(prefill_cache.shape, BF16),
            pltpu.VMEM((T, RES_DEV + G, RB, HD), BF16),
            pltpu.VMEM((G, RB, HD), BF16),
            pltpu.VMEM((G + RES_DEV, RB, HD), F32),
            pltpu.VMEM((NB, T, KVL, LW, HD), BF16),
            pltpu.VMEM((NB, T, KVL, LW, HD), BF16),
            pltpu.VMEM((NB, T, 8, LW), F32),
            pltpu.VMEM((NB, T, 8, LW), F32),
            pltpu.VMEM((LW, 128), F32),
            pltpu.VMEM((128, LW), F32),
            pltpu.VMEM((G, KVL, R, HD), BF16),
            pltpu.VMEM((G, KVL, R, HD), BF16),
            pltpu.VMEM((NB - 1, 8, LW), F32),
            pltpu.VMEM((G, 8, LW), F32),
            pltpu.VMEM((NB, 2, BATCH * STEPS, KVL * HD), F32),
            pltpu.VMEM((NB * BATCH, RB, HD), F32),
            dma((2,)),
            dma((G,)),
            dma((G,)),
            dma((T,)),
            dma((T,)),
            dma((G, T)),
            dma((G, T)),
            dma((NB, T)),
            dma((NB, T)),
            dma((NB, T)),
            dma((NB, T)),
            dma((G,)),
            dma((G,)),
            dma((G,)),
            dma((G,)),
        ],
        compiler_params=pltpu.CompilerParams(collective_id=0, has_side_effects=True),
    )(tbl, resident_kept, queries, new_entries, resident_cache, prefill_cache)


def solution(mesh):
    in_specs = (
        P("group", None, "tensor"),
        P("group", None, None),
        P("group", "tensor", None),
        P("group", "tensor", None),
        P(),
        P(),
        P(),
        P(),
    )
    out_specs = P("group", None, "tensor")
    return jax.shard_map(body, mesh=mesh, in_specs=in_specs, out_specs=out_specs, check_vma=False)
```

time: 172 us -> 53.9 us (0.31)
  waiting for transfers between devices: 83.4 us -> 0 us
  Pallas kernels: 0 us -> 48.5 us
  local copies, waits for them, and re-layouts: 43 us -> 1.69 us
  starting transfers between devices: 17.2 us -> 0 us
  blocking collectives: 13.1 us -> 0 us
  matrix products: 8.87 us -> 0 us
  other arithmetic: 5.57 us -> 3.59 us
    all_to_all x4 -> x0, waiting for transfers between devices: 83.4 us -> none  [the longest x1 65.7 us: body(): lax.all_to_all(outgoing.reshape(groups, per_pair, stride, features), 'gro...]
    pallas_call x0 -> x1, Pallas kernels: none -> 48.5 us  [body(): pl.pallas_call(functools.partial(kernel, G, T), out_shape=jax.ShapeDtypeS...]
    all_to_all x4 -> x0, starting transfers between devices: 17.2 us -> none  [the longest x1 6.49 us: body(): lax.all_to_all(outgoing.reshape(groups, per_pair, stride, features), 'gro...]
    gather x6 -> x0, local copies, waits for them, and re-layouts: 14.3 us -> none  [the longest x2 11.5 us: body(): arrived.reshape(groups * per_pair, stride, features)[arriving_rows]]
    scatter x4 -> x0, local copies, waits for them, and re-layouts: 13.8 us -> none  [the longest x1 10.9 us: body(): outgoing = jnp.zeros((groups * per_pair, stride, features), jnp.bfloat16)...]
    all_gather x1 -> x0, blocking collectives: 13.1 us -> none  [body(): asking = lax.all_gather(queries, 'tensor', axis=2, tiled=True)]
    dot_general x6 -> x0, matrix products: 8.87 us -> none  [the longest x2 4.38 us: partials(): jnp.einsum('rtkgd,rpkd->rtkgp', asked_rows, entries[:, :, 0], preferred_e...]
    broadcast_in_dim x4 -> x0, local copies, waits for them, and re-layouts: 4.92 us -> none  [the longest x1 2.49 us: body(): jnp.zeros((groups * per_pair, stride, features), jnp.bfloat16)]
  transfers between devices with their start and end apart: 4 -> 0, of which waited for: 4 -> 0; matrix products, arithmetic and copies ran while one was open for 13% -> 0% of each run, Pallas kernels for 0% -> 0%
where the time goes in v1:
time: 53.9 us; the launch traced here: 53.8 us
  Pallas kernels  48.5 us (90%)
  other arithmetic  3.59 us (7%)
  local copies, waits for them, and re-layouts  1.69 us (3%)
    pallas_call x1, Pallas kernels, body(): pl.pallas_call(functools.partial(kernel, G, T), out_shape=jax.ShapeDtypeS...  48.5 us
    unnamed x1, local copies, waits for them, and re-layouts  1.69 us

profile of v1, /device:TPU:0, one launch (start us, length us, event | category | flops | bytes accessed | tf_op | source)
XLA Modules:
  0.0 53.8 jit_solution(18384438190437661432)
XLA Ops:
  0.0 0.7 %and_select_fusion.1 = s32[64]{0:T(128)S(1)} fusion(s32[64]{0:T(128)} %param.14), kind=kLoop, calls=%fused_computation.14 | loop fusion | flops 704 | bytes 512 | tf_op jit(solution)/shard_map/jit(remainder)/select_n | solution.py:357
  0.7 0.7 %broadcast_add_fusion = (s32[64]{0:T(128)S(1)}, s32[64]{0:T(128)S(1)}) fusion(s32[64]{0:T(128)} %param.15), kind=kLoop, calls=%fused_computation.22 | loop fusion | flops 448 | bytes 768 | tf_op jit(solution)/shard_map/sub | solution.py:371
  1.3 0.7 %broadcast_compare_fusion = (pred[64]{0:T(512)(128)(4,1)S(1)}, s32[64]{0:T(128)S(1)}, pred[64]{0:T(512)(128)(4,1)S(1)}, s32[64]{0:T(128)S(1)}) fusion(s32[]{:T(128)S(6)} %axis_index.15, s32[64]{0:T(128)} %param.14, s32[64]{0:T(128)} %param.15), kind=kLoop, calls=%fused_computation.23 | loop fusion | flops 1600 | bytes 1156 | tf_op jit(solution)/shard_map/eq | solution.py:358
  2.0 0.1 select_reduce_fusion.3
  2.2 0.8 %select_reduce_fusion.2 = (s32[8]{0:T(128)S(1)}, s32[8]{0:T(128)S(1)}) fusion(s32[64]{0:T(128)S(1)} %and_select_fusion.1, s32[64]{0:T(128)S(1)} %get-tuple-element.16, pred[64]{0:T(512)(128)(4,1)S(1)} %get-tuple-element.9, s32[64]{0:T(128)} %param.13), kind=kLoop, calls=%fused_computation.3 | loop fusion | flops 3056 | bytes 896 | tf_op jit(solution)/shard_map/reduce_sum | solution.py:364
  3.0 0.6 %pad_add_fusion.tbl = s32[4,8]{1,0:T(4,128)} fusion(s32[1,8]{1,0:T(1,128)S(1)} %bitcast.5, s32[1,8]{1,0:T(1,128)S(1)} %bitcast.7, s32[1,8]{1,0:T(1,128)S(1)} %bitcast.6, s32[1,8]{1,0:T(1,128)S(1)} %bitcast.4), kind=kLoop, calls=%fused_computation.12 | loop fusion | flops 96 | bytes 256 | tf_op jit(solution)/shard_map/stack | solution.py:366
  3.6 48.5 %shard_map.82 = bf16[12,4,2048]{2,1,0:T(4,128)(2,1)} custom-call(s32[4,8]{1,0:T(4,128)} %pad_add_fusion.tbl, s32[32]{0:T(128)} %kept.1, bf16[12,4,2048]{2,1,0:T(4,128)(2,1)} %q_in.1, bf16[12,4,2048]{2,1,0:T(4,128)(2,1)} %new_in.1, bf16[4,128,2048]{2,1,0:T(8,128)(2,1)} %res_hbm.1, bf16[8,128,2048]{2,1,0:T(8,128)(2,1)} %pre_hbm.1), custom_call_target="tpu_custom_call" | custom-call | tf_op jit(solution)/shard_map/pallas_call | solution.py:399
  52.1 1.7 %copy.10 = bf16[12,4,2048]{2,1,0:T(4,128)(2,1)} copy(bf16[12,4,2048]{2,1,0:T(4,128)(2,1)} %shard_map.82) | data formatting | bytes 393216
  (1 shorter events, 0.0 us)

commit v2 on v1

--- a/solution.py
+++ b/solution.py
@@ -104,30 +104,30 @@
         )
 
     def c_zq(k):
-        return over_g(zq.at[k], qall.at[t, RES_DEV + k], zq_s.at[k], zq_r.at[k], peer_g(k))
+        return over_g(zq.at[k], qall.at[t, RES_DEV + k], zq_s.at[0], zq_r.at[k], peer_g(k))
 
     def c_rq(k):
         p = peer_t(k)
         own = qall.at[t, pl.ds(0, RES_DEV)]
-        return over_t(own, own, rq_s.at[k], rq_r.at[k], p)
+        return over_t(own, own, rq_s.at[0], rq_r.at[0], p)
 
     def c_fwd(k, n):
         own = qall.at[t, RES_DEV + k]
-        return over_t(own, own, f_s.at[k, n], f_r.at[k, n], peer_t(n))
+        return over_t(own, own, f_s.at[n], f_r.at[k], peer_t(n))
 
     def c_o(b, n):
         p = peer_t(n)
-        return over_t(obuf.at[b, p], rbuf.at[b, n], o_s.at[b, n], o_r.at[b, n], p)
+        return over_t(obuf.at[b, p], rbuf.at[b, n], o_s.at[b], o_r.at[b], p)
 
     def c_st(b, n):
         p = peer_t(n)
-        return over_t(sbuf.at[b, p], rstat.at[b, n], st_s.at[b, n], st_r.at[b, n], p)
+        return over_t(sbuf.at[b, p], rstat.at[b, n], st_s.at[b], st_r.at[b], p)
 
     def c_zo(k):
-        return over_g(zo.at[k], zro.at[k], zo_s.at[k], zo_r.at[k], from_g(k))
+        return over_g(zo.at[k], zro.at[k], zo_s.at[0], zo_r.at[k // BATCH], from_g(k))
 
     def c_zs(k):
-        return over_g(zs.at[k // BATCH], zrs.at[k], zs_s.at[k], zs_r.at[k], from_g(k))
+        return over_g(zs.at[k // BATCH], zrs.at[k], zs_s.at[0], zs_r.at[k // BATCH], from_g(k))
 
     load_res = pltpu.make_async_copy(res_hbm, res, cache_sem.at[0])
     load_pre = pltpu.make_async_copy(pre_hbm, pre, cache_sem.at[1])
@@ -147,7 +147,7 @@
         return stage[slot].astype(BF16)
 
     for k in range(G):
-        block = arranged(tbl[0, peer_g(k)], k)
+        block = arranged(tbl[peer_g(k)], k)
         zq[k] = block
         if k == 0:
             qall[t, RES_DEV] = block
@@ -165,7 +165,7 @@
     kv_col = pl.multiple_of((t * KVL * KVH) // (T * KVL) * HD, HD)
     for b in range(NB):
         for j in range(BATCH):
-            row = j if b == 0 else tbl[0, peer_g((b - 1) * BATCH + j)]
+            row = j if b == 0 else tbl[peer_g((b - 1) * BATCH + j)]
             lo = j * STEPS
             newk[b, 0, lo : lo + STEPS, :] = new_in[row, :, pl.ds(kv_col, KVL * HD)].astype(F32)
             newk[b, 1, lo : lo + STEPS, :] = new_in[
@@ -182,21 +182,39 @@
         usable = offset + lax.broadcasted_iota(jnp.int32, (R, pos), 1) < length
         stat = jnp.zeros((R, 128), F32)
         rows = pl.ds(pl.multiple_of(j * R, R), R)
-        for tt in range(T):
-            for i in range(KVL):
-                kv = (tt * KVL + i) * KVH // (T * KVL)
-                asked = qall[tt, slot, i * R : (i + 1) * R, :]
-                keys = cache[row, :, kv * HD : (kv + 1) * HD]
-                values = cache[row, :, half + kv * HD : half + (kv + 1) * HD]
-                scores = lax.dot_general(asked, keys, NT, preferred_element_type=F32) * SCALE
-                scores = jnp.where(usable, scores, NEG_FLOOR)
-                highest = jnp.max(scores, axis=1, keepdims=True)
-                weights = jnp.where(usable, jnp.exp(scores - highest), 0.0)
+        W = 2 if KVL % 2 == 0 else 1
+        units = [(tt, i) for tt in range(T) for i in range(0, KVL, W)]
+        all_scores = []
+        for tt, i in units:
+            kv = (tt * KVL + i) * KVH // (T * KVL)
+            asked = qall[tt, slot, i * R : (i + W) * R, :]
+            keys = jnp.concatenate(
+                [cache[row, :, (kv + w) * HD : (kv + w + 1) * HD] for w in range(W)], axis=0
+            )
+            scores = lax.dot_general(asked, keys, NT, preferred_element_type=F32)
+            all_scores.append(
+                [scores[w * R : (w + 1) * R, w * pos : (w + 1) * pos] * SCALE for w in range(W)]
+            )
+        all_weights = []
+        for (tt, i), scores in zip(units, all_scores):
+            rounded = []
+            for w in range(W):
+                masked = jnp.where(usable, scores[w], NEG_FLOOR)
+                highest = jnp.max(masked, axis=1, keepdims=True)
+                weights = jnp.where(usable, jnp.exp(masked - highest), 0.0)
                 total = jnp.sum(weights, axis=1, keepdims=True)
-                blended = jnp.dot(weights.astype(BF16), values, preferred_element_type=F32)
-                obuf[b, tt, i, rows, :] = blended.astype(BF16)
-                stat = jnp.where(lane == tt * SW + i, highest, stat)
-                stat = jnp.where(lane == tt * SW + KVL + i, total, stat)
+                rounded.append(weights.astype(BF16))
+                stat = jnp.where(lane == tt * SW + i + w, highest, stat)
+                stat = jnp.where(lane == tt * SW + KVL + i + w, total, stat)
+            all_weights.append(jnp.concatenate(rounded, axis=0))
+        for (tt, i), weights in zip(units, all_weights):
+            kv = (tt * KVL + i) * KVH // (T * KVL)
+            values = cache[row, :, half + kv * HD : half + (kv + W) * HD]
+            blended = jnp.dot(weights, values, preferred_element_type=F32)
+            for w in range(W):
+                obuf[b, tt, i + w, rows, :] = blended[
+                    w * R : (w + 1) * R, w * HD : (w + 1) * HD
+                ].astype(BF16)
         statbuf[rows, :] = stat
 
     def send_batch(b):
@@ -210,8 +228,9 @@
         rstat[b, 0] = sbuf[b, t]
 
     load_res.wait()
-    for n in range(1, T):
-        c_rq(n).wait_recv()
+    rest = pl.ds(1, T - 1)
+    q_rest = qall.at[rest, pl.ds(0, RES_DEV)]
+    over_t(q_rest, q_rest, rq_s.at[0], rq_r.at[0], t).wait_recv()
 
     @pl.loop(0, RES_DEV)
     def _(j):
@@ -225,17 +244,17 @@
         @pl.loop(0, BATCH)
         def _(j):
             k = (b - 1) * BATCH + j
-            for n in range(1, T):
-                c_fwd(k, n).wait_recv()
+            spread = qall.at[rest, RES_DEV + k]
+            over_t(spread, spread, f_s.at[0], f_r.at[k], t).wait_recv()
             source = from_g(k)
-            attend_slot(pre, tbl[1, source], tbl[2, source], RES_DEV + k, b, j)
+            held = tbl[G + source]
+            attend_slot(pre, held % MIG_DEV, held // MIG_DEV, RES_DEV + k, b, j)
 
         send_batch(b)
 
     def merged(b):
-        for n in range(1, T):
-            c_st(b, n).wait_recv()
-            c_o(b, n).wait_recv()
+        over_t(rstat.at[b, rest], rstat.at[b, rest], st_s.at[b], st_r.at[b], t).wait_recv()
+        over_t(rbuf.at[b, rest], rbuf.at[b, rest], o_s.at[b], o_r.at[b], t).wait_recv()
         tops = [rstat[b, n][:KVL] for n in range(T)]
         highest = functools.reduce(jnp.maximum, tops)
         total = jnp.zeros((KVL, LW), F32)
@@ -318,11 +337,12 @@
     for b in range(1, NB):
         lanes = lax.broadcasted_iota(jnp.int32, (8, LW), 1)
         stats = jnp.zeros((8, LW), F32)
+        first = (b - 1) * BATCH
+        came = pl.ds(max(first, 1), first + BATCH - max(first, 1))
+        over_g(zrs.at[came], zrs.at[came], zs_s.at[0], zs_r.at[b - 1], g).wait_recv()
+        over_g(zro.at[came], zro.at[came], zo_s.at[0], zo_r.at[b - 1], g).wait_recv()
         for j in range(BATCH):
             k = (b - 1) * BATCH + j
-            if k:
-                c_zs(k).wait_recv()
-                c_zo(k).wait_recv()
             stats = jnp.where(lanes // R == j, zrs[k], stats)
         blended = [
             jnp.concatenate(
@@ -332,45 +352,42 @@
         ]
         finish(b, stats[:KVL], stats[KVL:SW], blended, queries_of(b))
     for l in range(MIG_DEV):
-        put(RES_DEV + tbl[3, l], RES_DEV + l)
-
-    for k in range(1, G):
-        c_zq(k).wait_send()
-        c_zs(k).wait_send()
-        c_zo(k).wait_send()
+        k_of = 0
+        for k in range(1, G):
+            k_of = jnp.where(tbl[peer_g(k)] == RES_DEV + l, k, k_of)
+        put(RES_DEV + k_of, RES_DEV + l)
+
+    others = pl.ds(1, G - 1)
+    over_g(zq.at[others], zq.at[others], zq_s.at[0], zq_r.at[0], g).wait_send()
+    over_g(zrs.at[others], zrs.at[others], zs_s.at[0], zs_r.at[0], g).wait_send()
+    over_g(zo.at[others], zo.at[others], zo_s.at[0], zo_r.at[0], g).wait_send()
+    over_t(q_rest, q_rest, rq_s.at[0], rq_r.at[0], t).wait_send()
+    passed = qall.at[0, pl.ds(RES_DEV, G)]
     for n in range(1, T):
-        c_rq(n).wait_send()
-
-        @pl.loop(0, G)
-        def _(k):
-            c_fwd(k, n).wait_send()
-
-        @pl.loop(0, NB)
-        def _(b):
-            c_st(b, n).wait_send()
-            c_o(b, n).wait_send()
+        over_t(passed, passed, f_s.at[n], f_r.at[0], t).wait_send()
+    for b in range(NB):
+        over_t(rstat.at[b, rest], rstat.at[b, rest], st_s.at[b], st_r.at[b], t).wait_send()
+        over_t(rbuf.at[b, rest], rbuf.at[b, rest], o_s.at[b], o_r.at[b], t).wait_send()
 
 
 def routes(kept_tokens, prefill_slot, decode_slot, G):
     g = lax.axis_index("group")
-    dest_group, dest_row = decode_slot // PER_GROUP, decode_slot % PER_GROUP
-    home_group, home_row = prefill_slot // MIG_DEV, prefill_slot % MIG_DEV
-    arriving, leaving = dest_group == g, home_group == g
-    width = max(G, MIG_DEV)
-    every = jnp.arange(width, dtype=jnp.int32)[:, None]
-
-    def pick(key, wanted, value):
-        hit = (key[None] == every) & wanted[None]
-        return jnp.sum(jnp.where(hit, value[None], 0), axis=1)
-
-    return jnp.stack(
-        [
-            pick(home_group, arriving, dest_row),
-            pick(dest_group, leaving, home_row),
-            pick(dest_group, leaving, kept_tokens),
-            pick(dest_row - RES_DEV, arriving, (home_group - g + G) % G),
-        ]
+    shape = (2 * G, decode_slot.shape[0])
+    n = lax.broadcasted_iota(jnp.int32, shape, 0)
+    dest = jnp.broadcast_to(decode_slot[None], shape)
+    home = jnp.broadcast_to(prefill_slot[None], shape)
+    kept = jnp.broadcast_to(kept_tokens[None], shape)
+    dest_group, home_group = dest // PER_GROUP, home // MIG_DEV
+    first = n < G
+    hit = jnp.where(
+        first,
+        (dest_group == g) & (home_group == n),
+        (home_group == g) & (dest_group == n - G),
     )
+    value = jnp.where(
+        first, dest - dest_group * PER_GROUP, home - home_group * MIG_DEV + MIG_DEV * kept
+    )
+    return jnp.sum(jnp.where(hit, value, 0), axis=1)
 
 
 def body(
@@ -420,20 +437,20 @@
             pltpu.VMEM((NB, 2, BATCH * STEPS, KVL * HD), F32),
             pltpu.VMEM((NB * BATCH, RB, HD), F32),
             dma((2,)),
+            dma((1,)),
             dma((G,)),
+            dma((1,)),
+            dma((1,)),
+            dma((T,)),
             dma((G,)),
-            dma((T,)),
-            dma((T,)),
-            dma((G, T)),
-            dma((G, T)),
-            dma((NB, T)),
-            dma((NB, T)),
-            dma((NB, T)),
-            dma((NB, T)),
-            dma((G,)),
-            dma((G,)),
-            dma((G,)),
-            dma((G,)),
+            dma((NB,)),
+            dma((NB,)),
+            dma((NB,)),
+            dma((NB,)),
+            dma((1,)),
+            dma((NB - 1,)),
+            dma((1,)),
+            dma((NB - 1,)),
         ],
         compiler_params=pltpu.CompilerParams(collective_id=0, has_side_effects=True),
     )(tbl, resident_kept, queries, new_entries, resident_cache, prefill_cache)

time: 53.9 us -> 36.8 us (0.68)
  Pallas kernels: 48.5 us -> 31.5 us
    pallas_call x1, Pallas kernels: 48.5 us -> 31.5 us  [body(): pl.pallas_call(functools.partial(kernel, G, T), out_shape=jax.ShapeDtypeS...]
    eq x1 -> x0, other arithmetic: 0.69 us -> none  [routes(): arriving, leaving = (dest_group == g, home_group == g)]
    and x0 -> x1, other arithmetic: none -> 0.68 us  [routes(): dest_group, home_group = (dest // PER_GROUP, home // MIG_DEV)]
    sub x1 -> x3, other arithmetic: 0.67 us -> 1.35 us  [the longest x2 1.34 us: routes(): dest_group, home_group = (dest // PER_GROUP, home // MIG_DEV)]
    select_n x2 -> x0, other arithmetic: 0.68 us -> none  [the longest x1 0.66 us: routes(): home_group, home_row = (prefill_slot // MIG_DEV, prefill_slot % MIG_DEV)]
    another operation x1 -> x0, other arithmetic: 0.6 us -> none  [routes(): jnp.stack([pick(home_group, arriving, dest_row), pick(dest_group, leaving...]
    reduce_sum x2 -> x1, other arithmetic: 0.96 us -> 1.37 us  [routes(): return jnp.sum(jnp.where(hit, value, 0), axis=1)]
where the time goes in v2:
time: 36.8 us; the launch traced here: 36.6 us
  Pallas kernels  31.5 us (86%)
  other arithmetic  3.4 us (9%)
  local copies, waits for them, and re-layouts  1.69 us (5%)
    pallas_call x1, Pallas kernels, body(): pl.pallas_call(functools.partial(kernel, G, T), out_shape=jax.ShapeDtypeS...  31.5 us
    unnamed x1, local copies, waits for them, and re-layouts  1.69 us
    reduce_sum x1, other arithmetic, routes(): return jnp.sum(jnp.where(hit, value, 0), axis=1)  1.37 us
    sub x2, other arithmetic, routes(): dest_group, home_group = (dest // PER_GROUP, home // MIG_DEV)  1.34 us

profile of v2, /device:TPU:0, one launch (start us, length us, event | category | flops | bytes accessed | tf_op | source)
XLA Modules:
  0.0 36.6 jit_solution(3856425683711874466)
XLA Ops:
  0.0 0.7 %compare_and_fusion = (pred[64]{0:T(512)(128)(4,1)S(1)}, pred[64]{0:T(512)(128)(4,1)S(1)}) fusion(s32[64]{0:T(128)} %param.14, s32[64]{0:T(128)} %param.15), kind=kLoop, calls=%fused_computation.15 | loop fusion | flops 960 | bytes 640 | tf_op jit(solution)/shard_map/jit(floor_divide)/and | solution.py:380
  0.7 0.7 %broadcast_add_fusion.1 = (s32[64]{0:T(128)S(1)}, s32[64]{0:T(128)S(1)}) fusion(s32[64]{0:T(128)} %param.15), kind=kLoop, calls=%fused_computation.24 | loop fusion | flops 128 | bytes 768 | tf_op jit(solution)/shard_map/jit(floor_divide)/sub | solution.py:380
  1.4 0.7 %broadcast_add_fusion = (s32[64]{0:T(128)S(1)}, s32[64]{0:T(128)S(1)}, s32[64]{0:T(128)S(1)}) fusion(s32[64]{0:T(128)} %param.14, s32[64]{0:T(128)} %param.13), kind=kLoop, calls=%fused_computation.23 | loop fusion | flops 512 | bytes 1280 | tf_op jit(solution)/shard_map/jit(floor_divide)/sub | solution.py:380
  2.0 1.4 %fusion.3.tbl = s32[16]{0:T(128)} fusion(s32[64]{0:T(128)S(1)} %get-tuple-element.11, s32[64]{0:T(128)} %param.14, s32[64]{0:T(128)} %param.15, s32[16]{0:T(128)S(1)} %iota_add_fusion, s32[64]{0:T(128)S(1)} %get-tuple-element.8, s32[64]{0:T(128)S(1)} %get-tuple-element.7, s32[]{:T(128)S(6)} %axis_index.15, s32[64]{0:T(128)S(1)} %get-tuple-element.6, ...), kind=kLoop, calls=%fused_computation.9 | loop fusion | flops 17392 | bytes 2068 | tf_op jit(solution)/shard_map/reduce_sum | solution.py:390
  3.4 31.5 %shard_map.82 = bf16[12,4,2048]{2,1,0:T(4,128)(2,1)} custom-call(s32[16]{0:T(128)} %fusion.3.tbl, s32[32]{0:T(128)} %kept.1, bf16[12,4,2048]{2,1,0:T(4,128)(2,1)} %q_in.1, bf16[12,4,2048]{2,1,0:T(4,128)(2,1)} %new_in.1, bf16[4,128,2048]{2,1,0:T(8,128)(2,1)} %res_hbm.1, bf16[8,128,2048]{2,1,0:T(8,128)(2,1)} %pre_hbm.1), custom_call_target="tpu_custom_call" | custom-call | tf_op jit(solution)/shard_map/pallas_call | solution.py:416
  34.9 1.7 %copy.10 = bf16[12,4,2048]{2,1,0:T(4,128)(2,1)} copy(bf16[12,4,2048]{2,1,0:T(4,128)(2,1)} %shard_map.82) | data formatting | bytes 393216
  (2 shorter events, 0.0 us)

commit v3 on v2

--- a/solution.py
+++ b/solution.py
@@ -31,11 +31,13 @@
     T,
     tbl,
     kept,
-    q_in,
-    new_in,
+    q_hbm,
+    new_hbm,
     res_hbm,
     pre_hbm,
     out,
+    q_in,
+    new_in,
     res,
     pre,
     qall,
@@ -52,6 +54,8 @@
     zs,
     zrs,
     newk,
+    nstat,
+    nadd,
     fin,
     cache_sem,
     zq_s,
@@ -129,16 +133,20 @@
     def c_zs(k):
         return over_g(zs.at[k // BATCH], zrs.at[k], zs_s.at[0], zs_r.at[k // BATCH], from_g(k))
 
-    load_res = pltpu.make_async_copy(res_hbm, res, cache_sem.at[0])
-    load_pre = pltpu.make_async_copy(pre_hbm, pre, cache_sem.at[1])
-    load_res.start()
-    load_pre.start()
-
     barrier = pltpu.get_barrier_semaphore()
-    for k in range(1, G):
+    for k in range(G - 1, 0, -1):
         pl.semaphore_signal(barrier, inc=1, device_id=(peer_g(k), t), device_id_type=MESH)
     for k in range(1, T):
         pl.semaphore_signal(barrier, inc=1, device_id=(g, peer_t(k)), device_id_type=MESH)
+    load_q = pltpu.make_async_copy(q_hbm, q_in, cache_sem.at[2])
+    load_new = pltpu.make_async_copy(new_hbm, new_in, cache_sem.at[3])
+    load_res = pltpu.make_async_copy(res_hbm, res, cache_sem.at[0])
+    load_pre = pltpu.make_async_copy(pre_hbm, pre, cache_sem.at[1])
+    load_q.start()
+    load_new.start()
+    load_pre.start()
+    load_res.start()
+    load_q.wait()
 
     def arranged(row, slot):
         for h in range(HB):
@@ -162,6 +170,7 @@
     for n in range(1, T):
         c_fwd(0, n).start()
 
+    load_new.wait()
     kv_col = pl.multiple_of((t * KVL * KVH) // (T * KVL) * HD, HD)
     for b in range(NB):
         for j in range(BATCH):
@@ -171,6 +180,36 @@
             newk[b, 1, lo : lo + STEPS, :] = new_in[
                 row, :, pl.ds(pl.multiple_of(half + kv_col, HD), KVL * HD)
             ].astype(F32)
+
+    def queries_of(b):
+        return [
+            jnp.concatenate(
+                [
+                    (qall[t, j] if b == 0 else zq[(b - 1) * BATCH + j])[i * R : (i + 1) * R]
+                    for j in range(BATCH)
+                ],
+                axis=0,
+            )
+            for i in range(KVL)
+        ]
+
+    r16 = lax.broadcasted_iota(jnp.int32, (BATCH * STEPS, LW), 0)
+    lanes16 = lax.broadcasted_iota(jnp.int32, (BATCH * STEPS, LW), 1)
+    causal = (r16 // STEPS == lanes16 // R) & (r16 % STEPS <= lanes16 % STEPS)
+    for b in range(NB):
+        asked_b = queries_of(b)
+        for i in range(KVL):
+            keys = newk[b, 0, :, i * HD : (i + 1) * HD].astype(BF16)
+            values = newk[b, 1, :, i * HD : (i + 1) * HD].astype(BF16)
+            scores = lax.dot_general(keys, asked_b[i], NT, preferred_element_type=F32) * SCALE
+            scores = jnp.where(causal, scores, NEG_FLOOR)
+            top = jnp.max(scores, axis=0, keepdims=True)
+            weights = jnp.where(causal, jnp.exp(scores - top), 0.0)
+            nstat[b, i : i + 1, :] = top
+            nstat[b, KVL + i : KVL + i + 1, :] = jnp.sum(weights, axis=0, keepdims=True)
+            nadd[b, i] = lax.dot_general(
+                weights.astype(BF16), values, TN, preferred_element_type=F32
+            )
 
     for k in range(1, G):
         c_zq(k).wait_recv()
@@ -227,16 +266,7 @@
         rbuf[b, 0] = obuf[b, t]
         rstat[b, 0] = sbuf[b, t]
 
-    load_res.wait()
     rest = pl.ds(1, T - 1)
-    q_rest = qall.at[rest, pl.ds(0, RES_DEV)]
-    over_t(q_rest, q_rest, rq_s.at[0], rq_r.at[0], t).wait_recv()
-
-    @pl.loop(0, RES_DEV)
-    def _(j):
-        attend_slot(res, j, kept[g * RES_DEV + j], j, 0, j)
-
-    send_batch(0)
     load_pre.wait()
 
     @pl.loop(1, NB)
@@ -252,6 +282,15 @@
 
         send_batch(b)
 
+    load_res.wait()
+    q_rest = qall.at[rest, pl.ds(0, RES_DEV)]
+    over_t(q_rest, q_rest, rq_s.at[0], rq_r.at[0], t).wait_recv()
+
+    @pl.loop(0, RES_DEV)
+    def _(j):
+        attend_slot(res, j, kept[g * RES_DEV + j], j, 0, j)
+
+    send_batch(0)
     def merged(b):
         over_t(rstat.at[b, rest], rstat.at[b, rest], st_s.at[b], st_r.at[b], t).wait_recv()
         over_t(rbuf.at[b, rest], rbuf.at[b, rest], o_s.at[b], o_r.at[b], t).wait_recv()
@@ -272,29 +311,17 @@
             blended.append(sum_i)
         return highest, total, blended
 
-    def finish(b, highest, total, blended, asked):
-        r16 = lax.broadcasted_iota(jnp.int32, (BATCH * STEPS, LW), 0)
-        lanes = lax.broadcasted_iota(jnp.int32, (BATCH * STEPS, LW), 1)
-        causal = (r16 // STEPS == lanes // R) & (r16 % STEPS <= lanes % STEPS)
-        adds = []
-        for i in range(KVL):
-            keys = newk[b, 0, :, i * HD : (i + 1) * HD].astype(BF16)
-            values = newk[b, 1, :, i * HD : (i + 1) * HD].astype(BF16)
-            scores = lax.dot_general(keys, asked[i], NT, preferred_element_type=F32) * SCALE
-            scores = jnp.where(causal, scores, NEG_FLOOR)
-            top = jnp.maximum(highest[i : i + 1], jnp.max(scores, axis=0, keepdims=True))
-            weights = jnp.where(causal, jnp.exp(scores - top), 0.0)
-            carried = jnp.exp(highest[i : i + 1] - top)
-            inverse = 1.0 / (total[i : i + 1] * carried + jnp.sum(weights, axis=0, keepdims=True))
-            facbuf[i : i + 1, :] = carried
-            facbuf[KVL + i : KVL + i + 1, :] = inverse
-            adds.append(
-                lax.dot_general(weights.astype(BF16), values, TN, preferred_element_type=F32)
-            )
+    def finish(b, highest, total, blended):
+        new_top, new_total = nstat[b, 0:KVL], nstat[b, KVL:SW]
+        top = jnp.maximum(highest, new_top)
+        old_part, new_part = jnp.exp(highest - top), jnp.exp(new_top - top)
+        inverse = 1.0 / (total * old_part + new_total * new_part)
+        facbuf[0:KVL, :] = old_part * inverse
+        facbuf[KVL:SW, :] = new_part * inverse
         columns = facbuf[...].T
         for i in range(KVL):
-            done = blended[i] * columns[:, i : i + 1] + adds[i]
-            done = done * columns[:, KVL + i : KVL + i + 1]
+            done = blended[i] * columns[:, i : i + 1]
+            done = done + nadd[b, i] * columns[:, KVL + i : KVL + i + 1]
             for j in range(BATCH):
                 fin[b * BATCH + j, i * R : (i + 1) * R, :] = done[j * R : (j + 1) * R]
 
@@ -318,19 +345,7 @@
                 zrs[0] = zs[0]
                 zro[0] = zo[0]
 
-    def queries_of(b):
-        return [
-            jnp.concatenate(
-                [
-                    (qall[t, j] if b == 0 else zq[(b - 1) * BATCH + j])[i * R : (i + 1) * R]
-                    for j in range(BATCH)
-                ],
-                axis=0,
-            )
-            for i in range(KVL)
-        ]
-
-    finish(0, *merged(0), queries_of(0))
+    finish(0, *merged(0))
     for j in range(RES_DEV):
         put(j, j)
 
@@ -350,7 +365,7 @@
             )
             for i in range(KVL)
         ]
-        finish(b, stats[:KVL], stats[KVL:SW], blended, queries_of(b))
+        finish(b, stats[:KVL], stats[KVL:SW], blended)
     for l in range(MIG_DEV):
         k_of = 0
         for k in range(1, G):
@@ -415,10 +430,12 @@
     hbm = pl.BlockSpec(memory_space=pl.ANY)
     return pl.pallas_call(
         functools.partial(kernel, G, T),
-        out_shape=jax.ShapeDtypeStruct(queries.shape, BF16),
-        in_specs=[smem, smem, vmem, vmem, hbm, hbm],
+        out_shape=pltpu.VMEM(queries.shape, BF16),
+        in_specs=[smem, smem, hbm, hbm, hbm, hbm],
         out_specs=vmem,
         scratch_shapes=[
+            pltpu.VMEM(queries.shape, BF16),
+            pltpu.VMEM(new_entries.shape, BF16),
             pltpu.VMEM(resident_cache.shape, BF16),
             pltpu.VMEM(prefill_cache.shape, BF16),
             pltpu.VMEM((T, RES_DEV + G, RB, HD), BF16),
@@ -435,8 +452,10 @@
             pltpu.VMEM((NB - 1, 8, LW), F32),
             pltpu.VMEM((G, 8, LW), F32),
             pltpu.VMEM((NB, 2, BATCH * STEPS, KVL * HD), F32),
+            pltpu.VMEM((NB, 8, LW), F32),
+            pltpu.VMEM((NB, KVL, LW, HD), F32),
             pltpu.VMEM((NB * BATCH, RB, HD), F32),
-            dma((2,)),
+            dma((4,)),
             dma((1,)),
             dma((G,)),
             dma((1,)),

time: 36.8 us -> 33.1 us (0.90)
  Pallas kernels: 31.5 us -> 28.8 us
  local copies, waits for them, and re-layouts: 1.69 us -> 0.68 us
    pallas_call x1, Pallas kernels: 31.5 us -> 28.8 us  [body(): pl.pallas_call(functools.partial(kernel, G, T), out_shape=pltpu.VMEM(quer...]
    unnamed x1, local copies, waits for them, and re-layouts: 1.69 us -> 0.68 us
where the time goes in v3:
time: 33.1 us; the launch traced here: 32.9 us
  Pallas kernels  28.8 us (87%)
  other arithmetic  3.4 us (10%)
  local copies, waits for them, and re-layouts  0.68 us (2%)
    pallas_call x1, Pallas kernels, body(): pl.pallas_call(functools.partial(kernel, G, T), out_shape=pltpu.VMEM(quer...  28.8 us
    reduce_sum x1, other arithmetic, routes(): return jnp.sum(jnp.where(hit, value, 0), axis=1)  1.37 us
    sub x2, other arithmetic, routes(): dest_group, home_group = (dest // PER_GROUP, home // MIG_DEV)  1.34 us
    and x1, other arithmetic, routes(): dest_group, home_group = (dest // PER_GROUP, home // MIG_DEV)  0.68 us
    unnamed x1, local copies, waits for them, and re-layouts  0.68 us

profile of v3, /device:TPU:0, one launch (start us, length us, event | category | flops | bytes accessed | tf_op | source)
XLA Modules:
  0.0 32.9 jit_solution(1266856597724401477)
XLA Ops:
  0.0 0.7 %compare_and_fusion = (pred[64]{0:T(512)(128)(4,1)S(1)}, pred[64]{0:T(512)(128)(4,1)S(1)}) fusion(s32[64]{0:T(128)} %param.14, s32[64]{0:T(128)} %param.15), kind=kLoop, calls=%fused_computation.15 | loop fusion | flops 960 | bytes 640 | tf_op jit(solution)/shard_map/jit(floor_divide)/and | solution.py:395
  0.7 0.7 %broadcast_add_fusion.1 = (s32[64]{0:T(128)S(1)}, s32[64]{0:T(128)S(1)}) fusion(s32[64]{0:T(128)} %param.15), kind=kLoop, calls=%fused_computation.24 | loop fusion | flops 128 | bytes 768 | tf_op jit(solution)/shard_map/jit(floor_divide)/sub | solution.py:395
  1.4 0.7 %broadcast_add_fusion = (s32[64]{0:T(128)S(1)}, s32[64]{0:T(128)S(1)}, s32[64]{0:T(128)S(1)}) fusion(s32[64]{0:T(128)} %param.14, s32[64]{0:T(128)} %param.13), kind=kLoop, calls=%fused_computation.23 | loop fusion | flops 512 | bytes 1280 | tf_op jit(solution)/shard_map/jit(floor_divide)/sub | solution.py:395
  2.0 1.4 %fusion.3.tbl = s32[16]{0:T(128)} fusion(s32[64]{0:T(128)S(1)} %get-tuple-element.11, s32[64]{0:T(128)} %param.14, s32[64]{0:T(128)} %param.15, s32[16]{0:T(128)S(1)} %iota_add_fusion, s32[64]{0:T(128)S(1)} %get-tuple-element.8, s32[64]{0:T(128)S(1)} %get-tuple-element.7, s32[]{:T(128)S(6)} %axis_index.15, s32[64]{0:T(128)S(1)} %get-tuple-element.6, ...), kind=kLoop, calls=%fused_computation.9 | loop fusion | flops 17392 | bytes 2068 | tf_op jit(solution)/shard_map/reduce_sum | solution.py:405
  3.4 28.8 %shard_map.82 = bf16[12,4,2048]{2,1,0:T(4,128)(2,1)S(1)} custom-call(s32[16]{0:T(128)} %fusion.3.tbl, s32[32]{0:T(128)} %kept.1, bf16[12,4,2048]{2,1,0:T(4,128)(2,1)} %q_hbm.1, bf16[12,4,2048]{2,1,0:T(4,128)(2,1)} %new_hbm.1, bf16[4,128,2048]{2,1,0:T(8,128)(2,1)} %res_hbm.1, bf16[8,128,2048]{2,1,0:T(8,128)(2,1)} %pre_hbm.1), custom_call_target="tpu_custom_call" | custom-call | tf_op jit(solution)/shard_map/pallas_call | solution.py:431
  32.2 0.7 %copy.10 = bf16[12,4,2048]{2,1,0:T(4,128)(2,1)} copy(bf16[12,4,2048]{2,1,0:T(4,128)(2,1)S(1)} %shard_map.82) | data formatting | bytes 393216
  (2 shorter events, 0.0 us)

commit v4 on v3

--- a/solution.py
+++ b/solution.py
@@ -26,16 +26,36 @@
 TN = (((0,), (0,)), ((), ()))
 
 
+def fill_table(G, g, kept_v, home_v, dest_v, tab_v):
+    shape = (2 * G, dest_v.shape[1])
+    n = lax.broadcasted_iota(jnp.int32, shape, 0)
+    dest = jnp.broadcast_to(dest_v[...], shape)
+    home = jnp.broadcast_to(home_v[...], shape)
+    kept = jnp.broadcast_to(kept_v[...], shape)
+    dest_group, home_group = lax.div(dest, PER_GROUP), lax.div(home, MIG_DEV)
+    arriving = (dest_group == g) & (home_group == n)
+    leaving = (home_group == g) & (dest_group == n - G)
+    picked = jnp.where(arriving, dest - dest_group * PER_GROUP, 0)
+    held = home - home_group * MIG_DEV + MIG_DEV * kept
+    picked = picked + jnp.where(leaving, held, 0)
+    total = jnp.sum(picked, axis=1, keepdims=True)
+    tab_v[...] = jnp.broadcast_to(total, tab_v.shape)
+
+
 def kernel(
     G,
     T,
-    tbl,
+    kept_v,
+    home_v,
+    dest_v,
     kept,
     q_hbm,
     new_hbm,
     res_hbm,
     pre_hbm,
     out,
+    tab_v,
+    tab_s,
     q_in,
     new_in,
     res,
@@ -146,6 +166,10 @@
     load_new.start()
     load_pre.start()
     load_res.start()
+    fill_table(G, g, kept_v, home_v, dest_v, tab_v)
+    load_tab = pltpu.make_async_copy(tab_v, tab_s, cache_sem.at[4])
+    load_tab.start()
+    load_tab.wait()
     load_q.wait()
 
     def arranged(row, slot):
@@ -155,7 +179,7 @@
         return stage[slot].astype(BF16)
 
     for k in range(G):
-        block = arranged(tbl[peer_g(k)], k)
+        block = arranged(tab_s[peer_g(k), 0], k)
         zq[k] = block
         if k == 0:
             qall[t, RES_DEV] = block
@@ -174,7 +198,7 @@
     kv_col = pl.multiple_of((t * KVL * KVH) // (T * KVL) * HD, HD)
     for b in range(NB):
         for j in range(BATCH):
-            row = j if b == 0 else tbl[peer_g((b - 1) * BATCH + j)]
+            row = j if b == 0 else tab_s[peer_g((b - 1) * BATCH + j), 0]
             lo = j * STEPS
             newk[b, 0, lo : lo + STEPS, :] = new_in[row, :, pl.ds(kv_col, KVL * HD)].astype(F32)
             newk[b, 1, lo : lo + STEPS, :] = new_in[
@@ -277,7 +301,7 @@
             spread = qall.at[rest, RES_DEV + k]
             over_t(spread, spread, f_s.at[0], f_r.at[k], t).wait_recv()
             source = from_g(k)
-            held = tbl[G + source]
+            held = tab_s[G + source, 0]
             attend_slot(pre, held % MIG_DEV, held // MIG_DEV, RES_DEV + k, b, j)
 
         send_batch(b)
@@ -369,7 +393,7 @@
     for l in range(MIG_DEV):
         k_of = 0
         for k in range(1, G):
-            k_of = jnp.where(tbl[peer_g(k)] == RES_DEV + l, k, k_of)
+            k_of = jnp.where(tab_s[peer_g(k), 0] == RES_DEV + l, k, k_of)
         put(RES_DEV + k_of, RES_DEV + l)
 
     others = pl.ds(1, G - 1)
@@ -383,26 +407,6 @@
     for b in range(NB):
         over_t(rstat.at[b, rest], rstat.at[b, rest], st_s.at[b], st_r.at[b], t).wait_send()
         over_t(rbuf.at[b, rest], rbuf.at[b, rest], o_s.at[b], o_r.at[b], t).wait_send()
-
-
-def routes(kept_tokens, prefill_slot, decode_slot, G):
-    g = lax.axis_index("group")
-    shape = (2 * G, decode_slot.shape[0])
-    n = lax.broadcasted_iota(jnp.int32, shape, 0)
-    dest = jnp.broadcast_to(decode_slot[None], shape)
-    home = jnp.broadcast_to(prefill_slot[None], shape)
-    kept = jnp.broadcast_to(kept_tokens[None], shape)
-    dest_group, home_group = dest // PER_GROUP, home // MIG_DEV
-    first = n < G
-    hit = jnp.where(
-        first,
-        (dest_group == g) & (home_group == n),
-        (home_group == g) & (dest_group == n - G),
-    )
-    value = jnp.where(
-        first, dest - dest_group * PER_GROUP, home - home_group * MIG_DEV + MIG_DEV * kept
-    )
-    return jnp.sum(jnp.where(hit, value, 0), axis=1)
 
 
 def body(
@@ -423,7 +427,6 @@
     R = RB // KVL
     LW = BATCH * R
     NB = 1 + G // BATCH
-    tbl = routes(kept_tokens, prefill_slot, decode_slot, G)
     dma = pltpu.SemaphoreType.DMA
     vmem = pl.BlockSpec(memory_space=pltpu.VMEM)
     smem = pl.BlockSpec(memory_space=pltpu.SMEM)
@@ -431,9 +434,11 @@
     return pl.pallas_call(
         functools.partial(kernel, G, T),
         out_shape=pltpu.VMEM(queries.shape, BF16),
-        in_specs=[smem, smem, hbm, hbm, hbm, hbm],
+        in_specs=[vmem, vmem, vmem, smem, hbm, hbm, hbm, hbm],
         out_specs=vmem,
         scratch_shapes=[
+            pltpu.VMEM((2 * G, 128), jnp.int32),
+            pltpu.SMEM((2 * G, 128), jnp.int32),
             pltpu.VMEM(queries.shape, BF16),
             pltpu.VMEM(new_entries.shape, BF16),
             pltpu.VMEM(resident_cache.shape, BF16),
@@ -455,7 +460,7 @@
             pltpu.VMEM((NB, 8, LW), F32),
             pltpu.VMEM((NB, KVL, LW, HD), F32),
             pltpu.VMEM((NB * BATCH, RB, HD), F32),
-            dma((4,)),
+            dma((5,)),
             dma((1,)),
             dma((G,)),
             dma((1,)),
@@ -472,7 +477,12 @@
             dma((NB - 1,)),
         ],
         compiler_params=pltpu.CompilerParams(collective_id=0, has_side_effects=True),
-    )(tbl, resident_kept, queries, new_entries, resident_cache, prefill_cache)
+    )(
+        kept_tokens[None],
+        prefill_slot[None],
+        decode_slot[None],
+        resident_kept,
+        queries, new_entries, resident_cache, prefill_cache)
 
 
 def solution(mesh):

time: 33.1 us -> 29.8 us (0.900)
  other arithmetic: 3.4 us -> 0 us
    reduce_sum x1 -> x0, other arithmetic: 1.37 us -> none  [routes(): return jnp.sum(jnp.where(hit, value, 0), axis=1)]
    sub x3 -> x0, other arithmetic: 1.35 us -> none  [the longest x2 1.34 us: routes(): dest_group, home_group = (dest // PER_GROUP, home // MIG_DEV)]
    and x1 -> x0, other arithmetic: 0.68 us -> none  [routes(): dest_group, home_group = (dest // PER_GROUP, home // MIG_DEV)]
where the time goes in v4:
time: 29.8 us; the launch traced here: 29.6 us
  Pallas kernels  28.9 us (97%)
  local copies, waits for them, and re-layouts  0.68 us (2%)
    pallas_call x1, Pallas kernels, body(): pl.pallas_call(functools.partial(kernel, G, T), out_shape=pltpu.VMEM(quer...  28.9 us
    unnamed x1, local copies, waits for them, and re-layouts  0.68 us

profile of v4, /device:TPU:0, one launch (start us, length us, event | category | flops | bytes accessed | tf_op | source)
XLA Modules:
  0.0 29.6 jit_solution(13778070044198166667)
XLA Ops:
  0.0 28.9 %shard_map.82 = bf16[12,4,2048]{2,1,0:T(4,128)(2,1)S(1)} custom-call(s32[1,64]{1,0:T(1,128)} %bitcast.3, s32[1,64]{1,0:T(1,128)} %bitcast.4, s32[1,64]{1,0:T(1,128)} %bitcast.5, s32[32]{0:T(128)} %kept.1, bf16[12,4,2048]{2,1,0:T(4,128)(2,1)} %q_hbm.1, bf16[12,4,2048]{2,1,0:T(4,128)(2,1)} %new_hbm.1, bf16[4,128,2048]{2,1,0:T(8,128)(2,1)} %res_hbm.1, ...), custom_call_target="tpu_custom_call" | custom-call | tf_op jit(solution)/shard_map/pallas_call | solution.py:434
  28.9 0.7 %copy.10 = bf16[12,4,2048]{2,1,0:T(4,128)(2,1)} copy(bf16[12,4,2048]{2,1,0:T(4,128)(2,1)S(1)} %shard_map.82) | data formatting | bytes 393216

commit v5 on v4

--- a/solution.py
+++ b/solution.py
@@ -139,9 +139,12 @@
         own = qall.at[t, RES_DEV + k]
         return over_t(own, own, f_s.at[n], f_r.at[k], peer_t(n))
 
-    def c_o(b, n):
+    def c_o(b, j, n):
         p = peer_t(n)
-        return over_t(obuf.at[b, p], rbuf.at[b, n], o_s.at[b], o_r.at[b], p)
+        rows = pl.ds(pl.multiple_of(j * R, R), R)
+        return over_t(
+            obuf.at[b, p, :, rows], rbuf.at[b, n, :, rows], o_s.at[b], o_r.at[b], p
+        )
 
     def c_st(b, n):
         p = peer_t(n)
@@ -279,6 +282,8 @@
                     w * R : (w + 1) * R, w * HD : (w + 1) * HD
                 ].astype(BF16)
         statbuf[rows, :] = stat
+        for n in range(1, T):
+            c_o(b, j, n).start()
 
     def send_batch(b):
         turned = statbuf[...].T
@@ -286,7 +291,6 @@
             sbuf[b, tt] = turned[tt * SW : tt * SW + 8, :]
         for n in range(1, T):
             c_st(b, n).start()
-            c_o(b, n).start()
         rbuf[b, 0] = obuf[b, t]
         rstat[b, 0] = sbuf[b, t]
 

time: 29.8 us -> 29.4 us (0.987)
  Pallas kernels: 28.9 us -> 28.6 us
    pallas_call x1, Pallas kernels: 28.9 us -> 28.6 us  [body(): pl.pallas_call(functools.partial(kernel, G, T), out_shape=pltpu.VMEM(quer...]
where the time goes in v5:
time: 29.4 us; the launch traced here: 29.3 us
  Pallas kernels  28.6 us (97%)
  local copies, waits for them, and re-layouts  0.68 us (2%)
    pallas_call x1, Pallas kernels, body(): pl.pallas_call(functools.partial(kernel, G, T), out_shape=pltpu.VMEM(quer...  28.6 us
    unnamed x1, local copies, waits for them, and re-layouts  0.68 us

profile of v5, /device:TPU:0, one launch (start us, length us, event | category | flops | bytes accessed | tf_op | source)
XLA Modules:
  0.0 29.3 jit_solution(158352288912587101)
XLA Ops:
  0.0 28.6 %shard_map.82 = bf16[12,4,2048]{2,1,0:T(4,128)(2,1)S(1)} custom-call(s32[1,64]{1,0:T(1,128)} %bitcast.3, s32[1,64]{1,0:T(1,128)} %bitcast.4, s32[1,64]{1,0:T(1,128)} %bitcast.5, s32[32]{0:T(128)} %kept.1, bf16[12,4,2048]{2,1,0:T(4,128)(2,1)} %q_hbm.1, bf16[12,4,2048]{2,1,0:T(4,128)(2,1)} %new_hbm.1, bf16[4,128,2048]{2,1,0:T(8,128)(2,1)} %res_hbm.1, ...), custom_call_target="tpu_custom_call" | custom-call | tf_op jit(solution)/shard_map/pallas_call | solution.py:438
  28.6 0.7 %copy.10 = bf16[12,4,2048]{2,1,0:T(4,128)(2,1)} copy(bf16[12,4,2048]{2,1,0:T(4,128)(2,1)S(1)} %shard_map.82) | data formatting | bytes 393216
